TPU v7x, 128 devices: a whole 4x4x4 slice. The times are simulated.
128 devices in a mesh: dp: 4 (over y), expert: 32 (over x, z, core).
Axes of the slice: x: 4, y: 4, z: 4, core: 2. Of those that a mesh axis runs over, the one named last changes fastest.
Arguments:
- tokens: bfloat16 [4, 2048, 2048], P(None, ('dp', 'expert')), may hold values from -6 to 6
- routes: int32 [4, 2048, 8], P(None, ('dp', 'expert')), may hold values from 0 to 31, as said below
- gates: float32 [4, 2048, 8], P(None, ('dp', 'expert')), may hold values from 0.05 to 1
- gate_up: bfloat16 [32, 2048, 1536], P('expert'), may hold values from -0.125 to 0.125
- down: bfloat16 [32, 2048, 768], P('expert'), may hold values from -0.21875 to 0.21875
- expert_load: int32 [8, 32], P('dp'), may hold values from 1 to 4095
- swap_pairs: int32 [16, 2], replicated, may hold values from 0 to 31, as said below
Outputs:
- mixed: float32 [4, 2048, 2048], P(None, ('dp', 'expert'))
- moved_gate_up: bfloat16 [32, 2048, 1536], P('expert')
- moved_down: bfloat16 [32, 2048, 768], P('expert')
- slot_share: float32 [32], P('expert')
Inputs may be any that keep to these rules, and one draw needn't show every extreme that they name: `routes`: each row names 8 different experts. In every step the rows of one device name any expert at most 8 times, and in every step and every index of dp some expert is named exactly 8 times by the rows of every device. `swap_pairs`: the pairs name every slot exactly once.
All inputs are finite; a program needn't handle non-finite values.
Results may differ from a plain program's by a relative error of at most 0.0049.
Values may be sent and summed in bfloat16 or wider, within the bound.
A program may use at most 128 MiB of HBM per device.

v0:
```python
import math

import jax
import jax.numpy as jnp
from jax import lax
from jax.experimental import pallas as pl
from jax.experimental.pallas import tpu as pltpu
from jax.sharding import PartitionSpec as P

MESH = pl.DeviceIdType.MESH
STEPS, ROWS, WIDE, HID, TOPK = 4, 16, 2048, 768, 8
HALF = WIDE // 2
QUART = HALF // 2
CW = 384
CHUNKS = [(0, at) for at in range(0, 2 * HID, CW)] + [(1, at) for at in range(0, HID, CW)]
K = len(CHUNKS)
HB = 2

(
    W1, W2, W3, W4, W5, Y1, Y2, Y3, A1, A2, A3, A4, A5, C1, C2, R2, R3, R4, R5, R6, SR, WA, WB, WC, WD,
) = range(25)
X, Z = 0, 1
PLAN = [
    (W1, 3, Z), (A1, 0, X), (W1, 4, X), (W1, 2, X), (A1, 0, Z), (SR, 0, X), (W1, 4, Z), (A2, 0, X), (W1, 2, Z),
    (W2, 3, Z), (W1, 0, X), (A2, 0, Z), (W2, 4, X), (W2, 2, X), (A3, 0, X), (A1, 1, X), (A3, 0, Z), (W3, 3, Z),
    (WA, 0, X), (W3, 4, X), (W4, 3, Z), (W2, 2, Z), (W2, 0, X), (W3, 2, X), (W1, 3, X), (A4, 0, Z), (W4, 4, X),
    (W5, 3, Z), (A2, 1, X), (WB, 0, X), (A1, 1, Z), (A1, 3, X), (W4, 2, X), (W5, 4, X), (W2, 4, Z), (A1, 2, X),
    (W3, 0, X), (A4, 0, X), (A1, 2, Z), (Y1, 3, Z), (W3, 2, Z), (A5, 0, Z), (A2, 1, Z), (W4, 0, X), (W2, 3, X),
    (A3, 1, X), (W5, 2, X), (WC, 0, X), (A2, 3, X), (Y1, 4, X), (A3, 1, Z), (A5, 0, X), (W4, 2, Z), (A1, 3, Z),
    (W1, 0, Z), (W3, 4, Z), (W1, 1, Z), (A2, 2, X), (Y2, 3, Z), (WD, 0, X), (A2, 2, Z), (Y1, 2, X), (W5, 0, X),
    (C1, 0, X), (A4, 1, Z), (W4, 4, Z), (Y2, 4, X), (A4, 1, X), (W5, 2, Z), (C2, 0, X), (W3, 3, X), (W2, 0, Z),
    (A3, 2, X), (Y1, 0, X), (Y2, 2, X), (A5, 1, Z), (A3, 2, Z), (A5, 1, X), (W1, 1, X), (C2, 0, Z), (W2, 1, Z),
    (W5, 4, Z), (W1, 5, X), (W4, 3, X), (Y1, 2, Z), (W1, 5, Z), (A2, 3, Z), (W3, 0, Z), (C1, 1, X), (A4, 2, X),
    (Y1, 4, Z), (W2, 1, X), (A4, 2, Z), (W4, 0, Z), (A3, 3, X), (C2, 1, X), (W5, 3, X), (R2, 0, Z), (Y2, 0, X),
    (W2, 5, Z), (Y2, 2, Z), (W3, 1, Z), (A3, 3, Z), (A5, 2, Z), (A5, 2, X), (C2, 1, Z), (W4, 1, Z), (R2, 0, X),
    (W5, 0, Z), (R2, 1, X), (Y2, 4, Z), (W2, 5, X), (W3, 1, X), (A4, 3, X), (Y1, 3, X), (C1, 2, X), (W4, 1, X),
    (W3, 5, Z), (Y1, 0, Z), (C2, 2, X), (R2, 1, Z), (A4, 3, Z), (W5, 1, Z), (W3, 5, X), (W4, 5, Z), (Y2, 3, X),
    (A5, 3, X), (C2, 2, Z), (R2, 2, X), (R3, 0, Z), (A5, 3, Z), (W5, 1, X), (R3, 1, X), (Y2, 0, Z), (W4, 5, X),
    (R2, 2, Z), (Y1, 1, Z), (R3, 0, X), (W5, 5, Z), (C1, 3, X), (Y1, 1, X), (C2, 3, X), (W5, 5, X), (C2, 3, Z),
    (Y2, 1, Z), (R3, 2, Z), (R2, 3, X), (Y1, 5, Z), (R3, 2, X), (R2, 3, Z), (R4, 0, Z), (R3, 1, Z), (Y3, 4, X),
    (Y3, 2, X), (R3, 3, X), (Y1, 5, X), (R4, 2, Z), (Y2, 1, X), (R3, 3, Z), (Y3, 1, Z), (Y3, 3, X), (R4, 2, X),
    (R4, 1, X), (R4, 1, Z), (Y2, 5, Z), (R4, 0, X), (R5, 2, Z), (R4, 3, X), (R5, 0, Z), (R4, 3, Z), (R5, 2, X),
    (Y3, 2, Z), (R5, 1, Z), (R5, 0, X), (R5, 1, X), (Y2, 5, X), (R5, 3, X), (Y3, 4, Z), (R6, 0, Z), (R5, 3, Z),
    (Y3, 0, Z), (Y3, 1, X), (R6, 2, X), (R6, 2, Z), (R6, 1, Z), (Y3, 5, Z), (R6, 0, X), (Y3, 3, Z), (Y3, 0, X),
    (R6, 1, X), (R6, 3, X), (R6, 3, Z), (Y3, 5, X),
]

STAGES = [
    "W1", "W2", "W3", "W4", "W5", "Y1+", "Y1-", "Y2+", "Y2-",
    "A1+", "A1-", "A2+", "A2-", "A3+", "A3-", "A4+", "A4-", "A5",
    "R1", "R2+", "R2-", "R3+", "R3-", "R4+", "R4-", "R5+", "R5-",
    "WA", "WB", "WC", "L1", "L2", "L3",
]
AT = {name: i for i, name in enumerate(STAGES)}


def kernel(
    tok, gu, dn, routes_in, gates_in, load_in, pairs, mixed, out_gu, out_dn, share, *rest,
):
    full = [rest[2 * k : 2 * k + 2] for k in range(K)]
    (
        buf1, stage, buf3, xs, wgu, wdn, hid, part, sib, t0, t1, zz, u1, t2, v2, t3,
        routes, gates, load, wflat, wsend, wb1, wb2, wb3, wcol, lsend, lrecv, srcs, ss, rw, ry, ra, rr, misc,
    ) = rest[2 * K :]
    y = lax.axis_index("dp")
    e = lax.axis_index("expert")
    x, z, c = e // 8, (e // 2) % 4, e % 2

    def dev(dx=0, dz=0, dc=0, dy=0):
        return (
            lax.rem(y + dy, 4),
            (lax.rem(x + dx, 4) * 4 + lax.rem(z + dz, 4)) * 2 + lax.rem(c + dc, 2),
        )

    def first(h, o):
        return dev(dx=o) if h == 0 else dev(dz=o)

    def second(h, o):
        return dev(dz=o) if h == 0 else dev(dx=o)

    cf = (x, z)
    cg = (z, x)
    sent = {}

    def remote(name, src, dst, rsem, device):
        sent[name] = sent.get(name, 0) + math.prod(src.shape) * 2
        pltpu.make_async_remote_copy(
            src_ref=src, dst_ref=dst, send_sem=ss.at[AT[name]], recv_sem=rsem,
            device_id=device, device_id_type=MESH,
        ).start()

    def local(src, dst, sem):
        pltpu.make_async_copy(src, dst, sem).start()

    def arrived(ref, sem):
        pltpu.make_async_copy(ref, ref, sem).wait()

    def shift(base, o):
        return lax.rem(base + o, 4)

    weights = (gu, dn)
    moved = (out_gu, out_dn)

    def cols(k):
        return pl.ds(CHUNKS[k][1], CW)

    def region(k, h, yy):
        return moved[CHUNKS[k][0]].at[pl.ds(yy * 32 + h * 16, 16), :, cols(k)]

    def W1(k, h):
        for o in (1, 3, 2, 0):
            i = shift(cf[h], o)
            src = weights[CHUNKS[k][0]].at[pl.ds(y * 32 + h * 16 + 4 * i, 4), :, cols(k)]
            dst = buf1.at[k, h, cf[h]]
            if o:
                remote("W1", src, dst, rw.at[k, h, 0], first(h, o))
            else:
                local(src, dst, rw.at[k, h, 0])

    def W2(k, h):
        arrived(buf1.at[k, h], rw.at[k, h, 0])
        for o in (1, 3, 2, 0):
            src = buf1.at[k, h, :, shift(cg[h], o)]
            dst = full[k][h].at[pl.ds(c * 16 + cg[h] * 4, 4)]
            if o:
                remote("W2", src, dst, rw.at[k, h, 1], second(h, o))
            else:
                local(src, dst, rw.at[k, h, 1])

    def W3(k, h):
        mine = full[k][h].at[pl.ds(c * 16, 16)]
        arrived(mine, rw.at[k, h, 1])
        remote("W3", mine, mine, rw.at[k, h, 2], dev(dc=1))

    def W4(k, h):
        arrived(full[k][h].at[pl.ds((1 - c) * 16, 16)], rw.at[k, h, 2])
        for d in range(16):
            s = srcs[d]
            sx, sz, sc = s // 8, (s // 2) % 4, s % 2
            dx, dz = d // 4, d % 4
            if h == 0:
                stage[k, h, dz, dx] = full[k][h][sc * 16 + sz * 4 + sx]
            else:
                stage[k, h, dx, dz] = full[k][h][sc * 16 + sx * 4 + sz]
        for o in (1, 3, 2, 0):
            src = stage.at[k, h, shift(cg[h], o)]
            dst = buf3.at[k, h, cg[h]]
            if o:
                remote("W4", src, dst, rw.at[k, h, 3], second(h, o))
            else:
                local(src, dst, rw.at[k, h, 3])

    def W5(k, h):
        arrived(buf3.at[k, h], rw.at[k, h, 3])
        for o in (1, 3, 2, 0):
            src = buf3.at[k, h, :, shift(cf[h], o)]
            dst = moved[CHUNKS[k][0]].at[pl.ds(y * 32 + h * 16 + 4 * cf[h], 4), :, cols(k)]
            if o:
                remote("W5", src, dst, rw.at[k, h, 4], first(h, o))
            else:
                local(src, dst, rw.at[k, h, 4])

    def Y1(k, h):
        mine = region(k, h, y)
        arrived(mine, rw.at[k, h, 4])
        remote("Y1+", mine, mine, ry.at[k, h, 0], dev(dy=1))
        remote("Y1-", mine, mine, ry.at[k, h, 0], dev(dy=3))

    def Y2(k, h):
        arrived(buf1.at[pl.ds(0, 2), 0], ry.at[k, h, 0])
        up = region(k, h, shift(y, 3)).at[pl.ds(0, 8)]
        remote("Y2+", up, up, ry.at[k, h, 1], dev(dy=1))
        down = region(k, h, shift(y, 1)).at[pl.ds(8, 8)]
        remote("Y2-", down, down, ry.at[k, h, 1], dev(dy=3))

    def Y3(k, h):
        arrived(region(k, h, shift(y, 2)), ry.at[k, h, 1])

    def SR(_, __):
        def one(d, carry):
            slot = d * 2 + c
            total = jnp.int32(0)
            for i in range(16):
                a, b = pairs[0, i], pairs[1, i]
                total = total + jnp.where(a == slot, b, 0) + jnp.where(b == slot, a, 0)
            srcs[d] = total
            return carry

        lax.fori_loop(0, 16, one, 0)

    def side():
        arrived(routes, misc.at[6])
        arrived(gates, misc.at[7])
        arrived(load, misc.at[8])
        expert = lax.broadcasted_iota(jnp.int32, (32, ROWS), 0)
        for s in range(STEPS):
            g = gates[s]
            w = g / jnp.sum(g, axis=0, keepdims=True)
            r = routes[s]
            dense = jnp.zeros((32, ROWS), jnp.float32)
            for t in range(TOPK):
                dense = dense + jnp.where(r[t : t + 1] == expert, w[t : t + 1], 0.0)
            wflat[0:32, s * ROWS : (s + 1) * ROWS] = dense
        for d in range(32):
            wsend[d // 8, (d // 2) % 4, d % 2] = wflat[d : d + 1]
        lsend[...] = jnp.zeros((8, 128), jnp.int32)
        lsend[0:2, 0:32] = load[...]

    def WA(_, __):
        side()
        for o in (1, 3, 2):
            remote("WA", wsend.at[shift(x, o)], wb1.at[x], misc.at[0], dev(dx=o))
        local(wsend.at[x], wb1.at[x], misc.at[0])
        for o in (1, 2, 3):
            remote("L%d" % o, lsend, lrecv.at[y], misc.at[3], dev(dy=o))
        local(lsend, lrecv.at[y], misc.at[3])

    def WB(_, __):
        arrived(wb1, misc.at[0])
        for o in (1, 3, 2):
            remote("WB", wb1.at[:, shift(z, o)], wb2.at[:, z], misc.at[1], dev(dz=o))
        local(wb1.at[:, z], wb2.at[:, z], misc.at[1])

    def WC(_, __):
        arrived(wb2, misc.at[1])
        remote("WC", wb2.at[:, :, 1 - c], wb3.at[c], misc.at[2], dev(dc=1))
        local(wb2.at[:, :, c], wb3.at[c], misc.at[2])

    def WD(_, __):
        arrived(wb3, misc.at[2])
        wflat[...] = jnp.zeros((128, 128), jnp.float32)
        for d in range(32):
            wflat[d : d + 1] = wb3[d // 16, (d // 4) % 4, d % 4]
        wcol[...] = jnp.transpose(wflat[...])
        arrived(lrecv, misc.at[3])
        counts = jnp.sum(jnp.sum(lrecv[...], axis=0), axis=0, keepdims=True)
        lane = lax.broadcasted_iota(jnp.int32, (1, 128), 1)
        mine = jnp.int32(0)
        for i in range(16):
            a, b = pairs[0, i], pairs[1, i]
            mine = mine + jnp.where(a == e, b, 0) + jnp.where(b == e, a, 0)
        asf = counts.astype(jnp.float32)
        own = jnp.sum(jnp.where(lane == mine, asf, 0.0))
        share[0] = own / (jnp.sum(asf) / 32.0)

    def at_f(s, h, i):
        return xs.at[s, h, c, i, z] if h == 0 else xs.at[s, h, c, x, i]

    def line(s, h, i):
        return xs.at[s, h, c, :, i] if h == 0 else xs.at[s, h, c, i]

    LO, HI = pl.ds(0, QUART), pl.ds(QUART, QUART)

    def A1(s, h):
        src = tok.at[s, :, pl.ds(h * HALF, HALF)]
        dst = xs.at[s, h, c, x, z]
        remote("A1+", src, dst, ra.at[s, h, 0], first(h, 1))
        remote("A1-", src, dst, ra.at[s, h, 0], first(h, 3))
        local(src, dst, ra.at[s, h, 0])

    def A2(s, h):
        arrived(xs.at[s, h, 0, 0, pl.ds(0, 3)], ra.at[s, h, 0])
        lo = at_f(s, h, shift(cf[h], 3)).at[:, LO]
        remote("A2+", lo, lo, ra.at[s, h, 1], first(h, 1))
        hi = at_f(s, h, shift(cf[h], 1)).at[:, HI]
        remote("A2-", hi, hi, ra.at[s, h, 1], first(h, 3))

    def A3(s, h):
        arrived(at_f(s, h, shift(cf[h], 2)), ra.at[s, h, 1])
        mine = line(s, h, cg[h])
        remote("A3+", mine, mine, ra.at[s, h, 2], second(h, 1))
        remote("A3-", mine, mine, ra.at[s, h, 2], second(h, 3))

    def A4(s, h):
        arrived(xs.at[s, h, 0, pl.ds(0, 2)], ra.at[s, h, 2])
        lo = line(s, h, shift(cg[h], 3)).at[:, :, LO]
        remote("A4+", lo, lo, ra.at[s, h, 3], second(h, 1))
        hi = line(s, h, shift(cg[h], 1)).at[:, :, HI]
        remote("A4-", hi, hi, ra.at[s, h, 3], second(h, 3))

    def A5(s, h):
        arrived(line(s, h, shift(cg[h], 2)), ra.at[s, h, 3])
        mine = xs.at[s, h, c]
        remote("A5", mine, mine, ra.at[s, h, 4], dev(dc=1))

    loaded = []

    def C1(s, _):
        if not loaded:
            loaded.append(1)
            arrived(wgu, misc.at[4])
            arrived(wdn, misc.at[5])
        for h in (0, 1):
            arrived(xs.at[s, h, 1 - c], ra.at[s, h, 4])

        def tile(n, carry):
            at = pl.multiple_of(n * 256, 256)
            g = jnp.zeros((512, 256), jnp.float32)
            u = jnp.zeros((512, 256), jnp.float32)
            for h in (0, 1):
                rows = xs[s, h].reshape(512, HALF)
                g = g + jnp.dot(
                    rows,
                    wgu[h * 64 : (h + 1) * 64, :, pl.ds(at, 256)].reshape(HALF, 256),
                    preferred_element_type=jnp.float32,
                )
                u = u + jnp.dot(
                    rows,
                    wgu[h * 64 : (h + 1) * 64, :, pl.ds(pl.multiple_of(at + HID, 256), 256)].reshape(HALF, 256),
                    preferred_element_type=jnp.float32,
                )
            hid[s % HB, :, pl.ds(at, 256)] = (g / (1.0 + jnp.exp(-g)) * u).astype(jnp.bfloat16)
            return carry

        lax.fori_loop(0, 3, tile, 0)

    def C2(s, h):
        def tile(j, carry):
            at = pl.multiple_of(j * QUART, QUART)
            o = lax.dot_general(
                hid[s % HB],
                wdn[pl.ds(h * 64 + j * 32, 32)].reshape(QUART, HID),
                (((1,), (1,)), ((), ())),
                preferred_element_type=jnp.float32,
            )
            for d in range(32):
                w = wcol[s * ROWS : (s + 1) * ROWS, d : d + 1]
                piece = (o[d * ROWS : (d + 1) * ROWS] * w).astype(jnp.bfloat16)
                part[s, h, d // 16, (d // 4) % 4, d % 4, :, pl.ds(at, QUART)] = piece
            return carry

        lax.fori_loop(0, 2, tile, 0)
        remote("R1", part.at[s, h, 1 - c], sib.at[s, h], rr.at[s, h, 0], dev(dc=1))

    def f32(v):
        return v.astype(jnp.float32)

    def b16(v):
        return v.astype(jnp.bfloat16)

    def chip(s, h, i):
        if h == 0:
            return f32(part[s, h, c, i]) + f32(sib[s, h, i])
        return f32(part[s, h, c, :, i]) + f32(sib[s, h, :, i])

    def mine(s, h, i):
        return part.at[s, h, c, i] if h == 0 else part.at[s, h, c, :, i]

    def keep(s, h, i, cut, value):
        if h == 0:
            part[s, h, c, i, :, :, cut] = b16(value)
        else:
            part[s, h, c, :, i, :, cut] = b16(value)

    def R2(s, h):
        arrived(sib.at[s, h], rr.at[s, h, 0])
        i = shift(cf[h], 2)
        keep(s, h, i, slice(0, HALF), chip(s, h, i))
        remote("R2+", mine(s, h, i).at[:, :, LO], t0.at[s, h, :, :, LO], rr.at[s, h, 1], first(h, 1))
        remote("R2-", mine(s, h, i).at[:, :, HI], t0.at[s, h, :, :, HI], rr.at[s, h, 1], first(h, 3))

    def R3(s, h):
        arrived(t0.at[s, h], rr.at[s, h, 1])
        i = shift(cf[h], 1)
        v = chip(s, h, i)
        keep(s, h, i, slice(0, QUART), v[:, :, 0:QUART] + f32(t0[s, h, :, :, 0:QUART]))
        keep(s, h, i, slice(QUART, HALF), v[:, :, QUART:HALF])
        remote("R3+", mine(s, h, i), t1.at[s, h, 0], rr.at[s, h, 2], first(h, 1))
        i = shift(cf[h], 3)
        v = chip(s, h, i)
        keep(s, h, i, slice(0, QUART), v[:, :, 0:QUART])
        keep(s, h, i, slice(QUART, HALF), v[:, :, QUART:HALF] + f32(t0[s, h, :, :, QUART:HALF]))
        remote("R3-", mine(s, h, i), t1.at[s, h, 1], rr.at[s, h, 2], first(h, 3))

    def R4(s, h):
        arrived(t1.at[s, h], rr.at[s, h, 2])
        zz[s, h] = chip(s, h, cf[h]) + f32(t1[s, h, 0]) + f32(t1[s, h, 1])
        u1[s, h] = b16(zz[s, h, shift(cg[h], 2)])
        remote("R4+", u1.at[s, h, :, LO], t2.at[s, h, :, LO], rr.at[s, h, 3], second(h, 1))
        remote("R4-", u1.at[s, h, :, HI], t2.at[s, h, :, HI], rr.at[s, h, 3], second(h, 3))

    def R5(s, h):
        arrived(t2.at[s, h], rr.at[s, h, 3])
        v = zz[s, h, shift(cg[h], 1)]
        v2[s, h, 0, :, 0:QUART] = b16(v[:, 0:QUART] + f32(t2[s, h, :, 0:QUART]))
        v2[s, h, 0, :, QUART:HALF] = b16(v[:, QUART:HALF])
        remote("R5+", v2.at[s, h, 0], t3.at[s, h, 0], rr.at[s, h, 4], second(h, 1))
        v = zz[s, h, shift(cg[h], 3)]
        v2[s, h, 1, :, 0:QUART] = b16(v[:, 0:QUART])
        v2[s, h, 1, :, QUART:HALF] = b16(v[:, QUART:HALF] + f32(t2[s, h, :, QUART:HALF]))
        remote("R5-", v2.at[s, h, 1], t3.at[s, h, 1], rr.at[s, h, 4], second(h, 3))

    def R6(s, h):
        arrived(t3.at[s, h], rr.at[s, h, 4])
        mixed[s, :, h * HALF : (h + 1) * HALF] = zz[s, h, cg[h]] + f32(t3[s, h, 0]) + f32(t3[s, h, 1])

    bar = pltpu.get_barrier_semaphore()
    peers = [dev(dc=1)]
    for o in (1, 2, 3):
        peers += [dev(dx=o), dev(dz=o), dev(dy=o)]
    for peer in peers:
        pl.semaphore_signal(bar, inc=1, device_id=peer, device_id_type=MESH)
    for n, (src, dst) in enumerate(((routes_in, routes), (gates_in, gates), (load_in, load))):
        local(src, dst, misc.at[6 + n])
    pl.semaphore_wait(bar, len(peers))

    tasks = (
        W1, W2, W3, W4, W5, Y1, Y2, Y3, A1, A2, A3, A4, A5, C1, C2, R2, R3, R4, R5, R6, SR, WA, WB, WC, WD,
    )
    for number, item in enumerate(PLAN):
        stage_of, index, half = item
        tasks[stage_of](index, half)
        if number == 8:
            local(gu, wgu, misc.at[4])
            local(dn, wdn, misc.at[5])

    total = dict(
        {name: buf1.at[:, :, pl.ds(0, 3)] for name in ("W1", "W2", "W4", "W5")},
        **{name: buf1 for name in ("W3", "Y1+", "Y1-")},
        **{name: buf1.at[:, 0] for name in ("Y2+", "Y2-")},
        **{name: u1 for name in ("A1+", "A1-")},
        **{name: u1.at[:, :, :, LO] for name in ("A2+", "A2-", "R4+", "R4-")},
        **{name: t0 for name in ("A3+", "A3-", "R3+", "R3-")},
        **{name: t0.at[:, :, :, :, LO] for name in ("A4+", "A4-", "R2+", "R2-")},
        **{name: sib for name in ("A5", "R1")},
        **{name: u1 for name in ("R5+", "R5-")},
        WA=wsend.at[pl.ds(0, 3)], WB=wb1.at[:, pl.ds(0, 3)], WC=wb3.at[0],
        L1=lsend, L2=lsend, L3=lsend,
    )
    for name in sent:
        assert math.prod(total[name].shape) * 2 == sent[name], name
        arrived(total[name], ss.at[AT[name]])


def on_device(tokens, routes, gates, gate_up, down, expert_load, swap_pairs):
    hbm = pl.BlockSpec(memory_space=pltpu.HBM)
    vmem = pl.BlockSpec(memory_space=pltpu.VMEM)
    smem = pl.BlockSpec(memory_space=pltpu.SMEM)
    bf, f = jnp.bfloat16, jnp.float32
    sem = pltpu.SemaphoreType.DMA
    shapes = (
        jax.ShapeDtypeStruct((STEPS, ROWS, WIDE), f),
        jax.ShapeDtypeStruct((128, 16, 2 * HID), bf),
        jax.ShapeDtypeStruct((128, 16, HID), bf),
        jax.ShapeDtypeStruct((1,), f),
    )
    mixed, gu, dn, share = pl.pallas_call(
        kernel,
        out_shape=(pltpu.VMEM(shapes[0].shape, f), pltpu.VMEM(shapes[1].shape, bf), pltpu.VMEM(shapes[2].shape, bf), shapes[3]),
        in_specs=[hbm, hbm, hbm, hbm, hbm, hbm, smem],
        out_specs=(vmem, vmem, vmem, smem),
        scratch_shapes=[
            *[pltpu.VMEM((32, 16, CW), bf)] * (2 * K),
            pltpu.VMEM((K, 2, 4, 4, 16, CW), bf),
            pltpu.VMEM((K, 2, 4, 4, 16, CW), bf),
            pltpu.VMEM((K, 2, 4, 4, 16, CW), bf),
            pltpu.VMEM((STEPS, 2, 2, 4, 4, ROWS, HALF), bf),
            pltpu.VMEM((128, 16, 2 * HID), bf),
            pltpu.VMEM((128, 16, HID), bf),
            pltpu.VMEM((HB, 512, HID), bf),
            pltpu.VMEM((STEPS, 2, 2, 4, 4, ROWS, HALF), bf),
            pltpu.VMEM((STEPS, 2, 4, 4, ROWS, HALF), bf),
            pltpu.VMEM((STEPS, 2, 4, ROWS, HALF), bf),
            pltpu.VMEM((STEPS, 2, 2, 4, ROWS, HALF), bf),
            pltpu.VMEM((STEPS, 2, 4, ROWS, HALF), f),
            pltpu.VMEM((STEPS, 2, ROWS, HALF), bf),
            pltpu.VMEM((STEPS, 2, ROWS, HALF), bf),
            pltpu.VMEM((STEPS, 2, 2, ROWS, HALF), bf),
            pltpu.VMEM((STEPS, 2, 2, ROWS, HALF), bf),
            pltpu.VMEM((STEPS, TOPK, ROWS), jnp.int32),
            pltpu.VMEM((STEPS, TOPK, ROWS), f),
            pltpu.VMEM((2, 32), jnp.int32),
            pltpu.VMEM((128, 128), f),
            pltpu.VMEM((4, 4, 2, 1, 128), f),
            pltpu.VMEM((4, 4, 2, 1, 128), f),
            pltpu.VMEM((4, 4, 2, 1, 128), f),
            pltpu.VMEM((2, 4, 4, 1, 128), f),
            pltpu.VMEM((128, 128), f),
            pltpu.VMEM((8, 128), jnp.int32),
            pltpu.VMEM((4, 8, 128), jnp.int32),
            pltpu.SMEM((16,), jnp.int32),
            sem((len(STAGES),)),
            sem((K, 2, 5)),
            sem((K, 2, 2)),
            sem((STEPS, 2, 5)),
            sem((STEPS, 2, 5)),
            sem((9,)),
        ],
        compiler_params=pltpu.CompilerParams(
            collective_id=0, has_side_effects=True, vmem_limit_bytes=54 * 1024 * 1024
        ),
    )(
        tokens,
        gate_up.reshape(128, 16, 2 * HID),
        down.reshape(128, 16, HID),
        routes.transpose(0, 2, 1),
        gates.transpose(0, 2, 1),
        expert_load,
        swap_pairs.T,
    )
    return mixed, gu.reshape(1, WIDE, 2 * HID), dn.reshape(1, WIDE, HID), share


def solution(mesh):
    placed = (
        P(None, ("dp", "expert"), None),
        P(None, ("dp", "expert"), None),
        P(None, ("dp", "expert"), None),
        P("expert", None, None),
        P("expert", None, None),
        P("dp", None),
        P(),
    )
    return jax.shard_map(
        on_device,
        mesh=mesh,
        in_specs=placed,
        out_specs=(
            P(None, ("dp", "expert"), None),
            P("expert", None, None),
            P("expert", None, None),
            P("expert"),
        ),
        check_vma=False,
    )
```

profile of v0, /device:TPU:0, one launch (start us, length us, event | category | flops | bytes accessed | tf_op | source)
XLA Modules:
  0.0 118.5 jit_solution(16986565767023676566)
XLA Ops:
  0.6 111.0 %shard_map.102 = (f32[4,16,2048]{2,1,0:T(8,128)S(1)}, bf16[128,16,1536]{2,1,0:T(8,128)(2,1)S(1)}, bf16[128,16,768]{2,1,0:T(8,128)(2,1)S(1)}, f32[1]{0:T(128)}) custom-call(bf16[4,16,2048]{2,1,0:T(8,128)(2,1)} %tok.1, bf16[128,16,1536]{2,1,0:T(8,128)(2,1)} %bitcast.9, bf16[128,16,768]{2,1,0:T(8,128)(2,1)} %bitcast.10, s32[4,8,16]{2,1,0:T(8,128)} %bitcast.11, ...), custom_call_target="tpu_custom_call" | custom-call | tf_op jit(solution)/shard_map/pallas_call | solution.py:447
  111.7 0.8 copy.15
  112.4 2.7 %copy.16 = bf16[1,2048,1536]{2,1,0:T(8,128)(2,1)} copy(bf16[1,2048,1536]{2,1,0:T(8,128)(2,1)S(1)} %bitcast.7) | data formatting | bytes 12582912
  115.2 1.7 %copy.17 = bf16[1,2048,768]{2,1,0:T(8,128)(2,1)} copy(bf16[1,2048,768]{2,1,0:T(8,128)(2,1)S(1)} %bitcast.8) | data formatting | bytes 6291456
where the time goes:
time: 119 us
  Pallas kernels  111 us (93%)
  local copies, waits for them, and re-layouts  5.16 us (4%)
  between operations  2.33 us (2%)
    pallas_call x1, Pallas kernels, on_device(): pl.pallas_call(kernel, out_shape=(pltpu.VMEM(shapes[0].shape, f), pltpu.V...  111 us
    unnamed x3, local copies, waits for them, and re-layouts  5.16 us

commit v1 on v0

--- a/solution.py
+++ b/solution.py
@@ -430,6 +430,19 @@
     for name in sent:
         assert math.prod(total[name].shape) * 2 == sent[name], name
         arrived(total[name], ss.at[AT[name]])
+
+
+def copy_out(m_in, g_in, d_in, s_in, m_out, g_out, d_out, s_out, sems):
+    pairs = [(m_in, m_out)]
+    for i in range(4):
+        cut = pl.ds(32 * i, 32)
+        pairs += [(g_in.at[cut], g_out.at[cut]), (d_in.at[cut], d_out.at[cut])]
+    copies = [pltpu.make_async_copy(a, b, sems.at[n]) for n, (a, b) in enumerate(pairs)]
+    for copy in copies:
+        copy.start()
+    s_out[0] = s_in[0]
+    for copy in copies:
+        copy.wait()
 
 
 def on_device(tokens, routes, gates, gate_up, down, expert_load, swap_pairs):
@@ -498,6 +511,15 @@
         expert_load,
         swap_pairs.T,
     )
+    mixed, gu, dn = (pltpu.with_memory_space_constraint(v, pltpu.VMEM) for v in (mixed, gu, dn))
+    mixed, gu, dn, share = pl.pallas_call(
+        copy_out,
+        out_shape=shapes,
+        in_specs=[vmem, vmem, vmem, smem],
+        out_specs=(hbm, hbm, hbm, smem),
+        scratch_shapes=[sem((9,))],
+        compiler_params=pltpu.CompilerParams(vmem_limit_bytes=4 * 1024 * 1024),
+    )(mixed, gu, dn, share)
     return mixed, gu.reshape(1, WIDE, 2 * HID), dn.reshape(1, WIDE, HID), share
 
 

time: 119 us -> 117 us (0.983)
  local copies, waits for them, and re-layouts: 5.16 us -> 0 us
  Pallas kernels: 111 us -> 116 us
  between operations: 2.33 us -> 0.8 us
    unnamed x3 -> x0, local copies, waits for them, and re-layouts: 5.16 us -> none
    pallas_call x0 -> x1, Pallas kernels: none -> 4.99 us  [on_device(): pl.pallas_call(copy_out, out_shape=shapes, in_specs=[vmem, vmem, vmem, sm...]
where the time goes in v1:
time: 117 us
  Pallas kernels  116 us (99%)
    pallas_call x1, Pallas kernels, on_device(): pl.pallas_call(kernel, out_shape=(pltpu.VMEM(shapes[0].shape, f), pltpu.V...  111 us
    pallas_call x1, Pallas kernels, on_device(): pl.pallas_call(copy_out, out_shape=shapes, in_specs=[vmem, vmem, vmem, sm...  4.99 us

profile of v1, /device:TPU:0, one launch (start us, length us, event | category | flops | bytes accessed | tf_op | source)
XLA Modules:
  0.0 116.8 jit_solution(11850017691678668980)
XLA Ops:
  0.6 111.0 %shard_map.102 = (f32[4,16,2048]{2,1,0:T(8,128)S(1)}, bf16[128,16,1536]{2,1,0:T(8,128)(2,1)S(1)}, bf16[128,16,768]{2,1,0:T(8,128)(2,1)S(1)}, f32[1]{0:T(128)}) custom-call(bf16[4,16,2048]{2,1,0:T(8,128)(2,1)} %tok.1, bf16[128,16,1536]{2,1,0:T(8,128)(2,1)} %bitcast.7, bf16[128,16,768]{2,1,0:T(8,128)(2,1)} %bitcast.8, s32[4,8,16]{2,1,0:T(8,128)} %bitcast.9, ...), custom_call_target="tpu_custom_call" | custom-call | tf_op jit(solution)/shard_map/pallas_call | solution.py:460
  111.7 5.0 %shard_map.103 = (f32[4,16,2048]{2,1,0:T(8,128)}, bf16[128,16,1536]{2,1,0:T(8,128)(2,1)}, bf16[128,16,768]{2,1,0:T(8,128)(2,1)}, f32[1]{0:T(128)}) custom-call(f32[4,16,2048]{2,1,0:T(8,128)S(1)} %get-tuple-element.12.m_in, bf16[128,16,1536]{2,1,0:T(8,128)(2,1)S(1)} %get-tuple-element.13.g_in, bf16[128,16,768]{2,1,0:T(8,128)(2,1)S(1)} %get-tuple-element.14.d_in, ...), custom_call_target="tpu_custom_call" | custom-call | tf_op jit(solution)/shard_map/pallas_call | solution.py:515

commit v2 on v1

--- a/solution.py
+++ b/solution.py
@@ -60,7 +60,7 @@
     full = [rest[2 * k : 2 * k + 2] for k in range(K)]
     (
         buf1, stage, buf3, xs, wgu, wdn, hid, part, sib, t0, t1, zz, u1, t2, v2, t3,
-        routes, gates, load, wflat, wsend, wb1, wb2, wb3, wcol, lsend, lrecv, srcs, ss, rw, ry, ra, rr, misc,
+        routes, gates, load, wflat, wsend, wb1, wb2, wb3, wcol, lsend, lrecv, srcs, ss, rw, ry, ra, misc,
     ) = rest[2 * K :]
     y = lax.axis_index("dp")
     e = lax.axis_index("expert")
@@ -330,7 +330,7 @@
             return carry
 
         lax.fori_loop(0, 2, tile, 0)
-        remote("R1", part.at[s, h, 1 - c], sib.at[s, h], rr.at[s, h, 0], dev(dc=1))
+        remote("R1", part.at[s, h, 1 - c], sib.at[s, h], ra.at[s, h, 0], dev(dc=1))
 
     def f32(v):
         return v.astype(jnp.float32)
@@ -353,45 +353,45 @@
             part[s, h, c, :, i, :, cut] = b16(value)
 
     def R2(s, h):
-        arrived(sib.at[s, h], rr.at[s, h, 0])
+        arrived(sib.at[s, h], ra.at[s, h, 0])
         i = shift(cf[h], 2)
         keep(s, h, i, slice(0, HALF), chip(s, h, i))
-        remote("R2+", mine(s, h, i).at[:, :, LO], t0.at[s, h, :, :, LO], rr.at[s, h, 1], first(h, 1))
-        remote("R2-", mine(s, h, i).at[:, :, HI], t0.at[s, h, :, :, HI], rr.at[s, h, 1], first(h, 3))
+        remote("R2+", mine(s, h, i).at[:, :, LO], t0.at[s, h, :, :, LO], ra.at[s, h, 1], first(h, 1))
+        remote("R2-", mine(s, h, i).at[:, :, HI], t0.at[s, h, :, :, HI], ra.at[s, h, 1], first(h, 3))
 
     def R3(s, h):
-        arrived(t0.at[s, h], rr.at[s, h, 1])
+        arrived(t0.at[s, h], ra.at[s, h, 1])
         i = shift(cf[h], 1)
         v = chip(s, h, i)
         keep(s, h, i, slice(0, QUART), v[:, :, 0:QUART] + f32(t0[s, h, :, :, 0:QUART]))
         keep(s, h, i, slice(QUART, HALF), v[:, :, QUART:HALF])
-        remote("R3+", mine(s, h, i), t1.at[s, h, 0], rr.at[s, h, 2], first(h, 1))
+        remote("R3+", mine(s, h, i), t1.at[s, h, 0], ra.at[s, h, 2], first(h, 1))
         i = shift(cf[h], 3)
         v = chip(s, h, i)
         keep(s, h, i, slice(0, QUART), v[:, :, 0:QUART])
         keep(s, h, i, slice(QUART, HALF), v[:, :, QUART:HALF] + f32(t0[s, h, :, :, QUART:HALF]))
-        remote("R3-", mine(s, h, i), t1.at[s, h, 1], rr.at[s, h, 2], first(h, 3))
+        remote("R3-", mine(s, h, i), t1.at[s, h, 1], ra.at[s, h, 2], first(h, 3))
 
     def R4(s, h):
-        arrived(t1.at[s, h], rr.at[s, h, 2])
+        arrived(t1.at[s, h], ra.at[s, h, 2])
         zz[s, h] = chip(s, h, cf[h]) + f32(t1[s, h, 0]) + f32(t1[s, h, 1])
         u1[s, h] = b16(zz[s, h, shift(cg[h], 2)])
-        remote("R4+", u1.at[s, h, :, LO], t2.at[s, h, :, LO], rr.at[s, h, 3], second(h, 1))
-        remote("R4-", u1.at[s, h, :, HI], t2.at[s, h, :, HI], rr.at[s, h, 3], second(h, 3))
+        remote("R4+", u1.at[s, h, :, LO], t2.at[s, h, :, LO], ra.at[s, h, 3], second(h, 1))
+        remote("R4-", u1.at[s, h, :, HI], t2.at[s, h, :, HI], ra.at[s, h, 3], second(h, 3))
 
     def R5(s, h):
-        arrived(t2.at[s, h], rr.at[s, h, 3])
+        arrived(t2.at[s, h], ra.at[s, h, 3])
         v = zz[s, h, shift(cg[h], 1)]
         v2[s, h, 0, :, 0:QUART] = b16(v[:, 0:QUART] + f32(t2[s, h, :, 0:QUART]))
         v2[s, h, 0, :, QUART:HALF] = b16(v[:, QUART:HALF])
-        remote("R5+", v2.at[s, h, 0], t3.at[s, h, 0], rr.at[s, h, 4], second(h, 1))
+        remote("R5+", v2.at[s, h, 0], t3.at[s, h, 0], ra.at[s, h, 4], second(h, 1))
         v = zz[s, h, shift(cg[h], 3)]
         v2[s, h, 1, :, 0:QUART] = b16(v[:, 0:QUART])
         v2[s, h, 1, :, QUART:HALF] = b16(v[:, QUART:HALF] + f32(t2[s, h, :, QUART:HALF]))
-        remote("R5-", v2.at[s, h, 1], t3.at[s, h, 1], rr.at[s, h, 4], second(h, 3))
+        remote("R5-", v2.at[s, h, 1], t3.at[s, h, 1], ra.at[s, h, 4], second(h, 3))
 
     def R6(s, h):
-        arrived(t3.at[s, h], rr.at[s, h, 4])
+        arrived(t3.at[s, h], ra.at[s, h, 4])
         mixed[s, :, h * HALF : (h + 1) * HALF] = zz[s, h, cg[h]] + f32(t3[s, h, 0]) + f32(t3[s, h, 1])
 
     bar = pltpu.get_barrier_semaphore()
@@ -496,7 +496,6 @@
             sem((K, 2, 5)),
             sem((K, 2, 2)),
             sem((STEPS, 2, 5)),
-            sem((STEPS, 2, 5)),
             sem((9,)),
         ],
         compiler_params=pltpu.CompilerParams(

time: 117 us -> 117 us (level)
  no operation moved by 1% of the time
where the time goes in v2:
time: 117 us; the launch traced here: 116 us
  Pallas kernels  116 us (99%)
    pallas_call x1, Pallas kernels, on_device(): pl.pallas_call(kernel, out_shape=(pltpu.VMEM(shapes[0].shape, f), pltpu.V...  111 us
    pallas_call x1, Pallas kernels, on_device(): pl.pallas_call(copy_out, out_shape=shapes, in_specs=[vmem, vmem, vmem, sm...  4.99 us

profile of v2, /device:TPU:0, one launch (start us, length us, event | category | flops | bytes accessed | tf_op | source)
XLA Modules:
  0.0 116.4 jit_solution(4091133190341083936)
XLA Ops:
  0.6 110.7 %shard_map.102 = (f32[4,16,2048]{2,1,0:T(8,128)S(1)}, bf16[128,16,1536]{2,1,0:T(8,128)(2,1)S(1)}, bf16[128,16,768]{2,1,0:T(8,128)(2,1)S(1)}, f32[1]{0:T(128)}) custom-call(bf16[4,16,2048]{2,1,0:T(8,128)(2,1)} %tok.1, bf16[128,16,1536]{2,1,0:T(8,128)(2,1)} %bitcast.7, bf16[128,16,768]{2,1,0:T(8,128)(2,1)} %bitcast.8, s32[4,8,16]{2,1,0:T(8,128)} %bitcast.9, ...), custom_call_target="tpu_custom_call" | custom-call | tf_op jit(solution)/shard_map/pallas_call | solution.py:460
  111.3 5.0 %shard_map.103 = (f32[4,16,2048]{2,1,0:T(8,128)}, bf16[128,16,1536]{2,1,0:T(8,128)(2,1)}, bf16[128,16,768]{2,1,0:T(8,128)(2,1)}, f32[1]{0:T(128)}) custom-call(f32[4,16,2048]{2,1,0:T(8,128)S(1)} %get-tuple-element.12.m_in, bf16[128,16,1536]{2,1,0:T(8,128)(2,1)S(1)} %get-tuple-element.13.g_in, bf16[128,16,768]{2,1,0:T(8,128)(2,1)S(1)} %get-tuple-element.14.d_in, ...), custom_call_target="tpu_custom_call" | custom-call | tf_op jit(solution)/shard_map/pallas_call | solution.py:514
